TPU v7x, 128 devices: a whole 4x4x4 slice. The times are simulated.
128 devices in a mesh: dp: 16 (over x, y), expert: 8 (over z, core).
Axes of the slice: x: 4, y: 4, z: 4, core: 2. Of those that a mesh axis runs over, the one named last changes fastest.
Arguments:
- tokens: bfloat16 [2048, 4096], P('dp', 'expert'), may hold values from -6 to 6
- output_gradient: bfloat16 [2048, 4096], P('dp', 'expert'), may hold values from -6 to 6
- routing: int32 [2048, 2], P('dp'), may hold values from 0 to 7, all different within a row; in each aligned block of 128 rows (0 to 127, 128 to 255, ...) at most 96 rows name the same one
- router_gate_values: float32 [2048, 2], P('dp'), may hold values from 0.1 to 0.9
- gate_weight: bfloat16 [8, 7168, 4096], P('expert', 'dp'), may hold values from -0.09375 to 0.09375
- up_weight: bfloat16 [8, 7168, 4096], P('expert', 'dp'), may hold values from -0.09375 to 0.09375
- down_weight: bfloat16 [8, 7168, 4096], P('expert', 'dp'), may hold values from -0.0625 to 0.0625
- adapter_lower_gate: bfloat16 [8, 16, 4096], P('expert'), may hold values from -0.09375 to 0.09375
- adapter_upper_gate: bfloat16 [8, 7168, 16], P('expert', 'dp'), may hold values from -0.375 to 0.375
- adapter_lower_up: bfloat16 [8, 16, 4096], P('expert'), may hold values from -0.09375 to 0.09375
- adapter_upper_up: bfloat16 [8, 7168, 16], P('expert', 'dp'), may hold values from -0.375 to 0.375
- adapter_lower_down: bfloat16 [8, 16, 7168], P('expert', None, 'dp'), may hold values from -0.0625 to 0.0625
- adapter_upper_down: bfloat16 [8, 4096, 16], P('expert'), may hold values from -0.375 to 0.375
Outputs:
- grad_x: bfloat16 [2048, 4096], P('dp', 'expert')
- grad_lora_a_gate: float32 [8, 16, 4096], P('expert')
- grad_lora_b_gate: float32 [8, 7168, 16], P('expert', 'dp')
- grad_lora_a_up: float32 [8, 16, 4096], P('expert')
- grad_lora_b_up: float32 [8, 7168, 16], P('expert', 'dp')
- grad_lora_a_down: float32 [8, 16, 7168], P('expert', None, 'dp')
- grad_lora_b_down: float32 [8, 4096, 16], P('expert')
Inputs may be any that keep to these rules, and one draw needn't show every extreme that they name: `routing`: each row names two different experts. In the rows of one dp shard (aligned blocks of 128 rows) no expert is named by more than 96 rows, and in some blocks one expert is named by exactly 96 rows.
All inputs are finite; a program needn't handle non-finite values.
Results may differ from a plain program's by a relative error of at most 0.015.
Values may be sent and summed in bfloat16 or wider, within the bound.
A program may use at most 256 MiB of HBM per device.

v0:
```python
import jax
import jax.numpy as jnp
from jax import lax
from jax.sharding import PartitionSpec as P

ADAPTER_SCALE = 2.0
NUM_CHUNKS = 2
PART_COLS = 128


def contract_pair(left, right, left_axis, right_axis):
    return lax.dot_general(
        left, right, (((left_axis,), (right_axis,)), ((), ())), preferred_element_type=jnp.float32
    )


def slot_numbers(route_rows, experts):
    picked = (route_rows[:, :, None] == jnp.arange(experts, dtype=jnp.int32)[None, None, :]).astype(
        jnp.int32
    )
    per_token = jnp.sum(picked, axis=1)
    earlier = jnp.cumsum(per_token, axis=0) - per_token
    return jnp.sum(earlier[:, None, :] * picked, axis=2)


def slot_sources(route_rows, positions, experts, capacity):
    tokens_here, choose = route_rows.shape
    target = (route_rows * capacity + positions).reshape(-1)
    owners = jnp.repeat(jnp.arange(tokens_here, dtype=jnp.int32), choose)
    member_ids = jnp.tile(jnp.arange(choose, dtype=jnp.int32), tokens_here)
    source = jnp.full((experts * capacity,), tokens_here, jnp.int32).at[target].set(owners)
    member = jnp.zeros((experts * capacity,), jnp.int32).at[target].set(member_ids)
    return (source, member)


def rows_backward_pass(input_rows, output_gradient_rows, params):
    (
        gate_weight,
        up_weight,
        down_weight,
        a_gate,
        gate_adapter_upper,
        a_up,
        up_adapter_upper,
        down_adapter_lower,
        b_down,
    ) = params
    gate_projected_lower = contract_pair(a_gate, input_rows, 1, 1).astype(jnp.bfloat16)
    up_projected_lower = contract_pair(a_up, input_rows, 1, 1).astype(jnp.bfloat16)
    gate_preactivation = contract_pair(
        gate_weight, input_rows, 1, 1
    ) + ADAPTER_SCALE * contract_pair(gate_adapter_upper, gate_projected_lower, 1, 0)
    up_preactivation = contract_pair(up_weight, input_rows, 1, 1) + ADAPTER_SCALE * contract_pair(
        up_adapter_upper, up_projected_lower, 1, 0
    )
    sigmoid_gate = jax.nn.sigmoid(gate_preactivation)
    silu_gate = gate_preactivation * sigmoid_gate
    hidden_units = (silu_gate * up_preactivation).astype(jnp.bfloat16)
    down_projected_lower = contract_pair(b_down, output_gradient_rows, 0, 1).astype(jnp.bfloat16)
    hidden_gradient = contract_pair(
        down_weight, output_gradient_rows, 1, 1
    ) + ADAPTER_SCALE * contract_pair(down_adapter_lower, down_projected_lower, 0, 0)
    gate_gradient = (
        hidden_gradient
        * up_preactivation
        * sigmoid_gate
        * (1.0 + gate_preactivation * (1.0 - sigmoid_gate))
    ).astype(jnp.bfloat16)
    up_gradient = (hidden_gradient * silu_gate).astype(jnp.bfloat16)
    gate_partial = contract_pair(gate_adapter_upper, gate_gradient, 0, 0).astype(jnp.bfloat16)
    up_partial = contract_pair(up_adapter_upper, up_gradient, 0, 0).astype(jnp.bfloat16)
    down_partial = contract_pair(down_adapter_lower, hidden_units, 1, 0).astype(jnp.bfloat16)
    paired_partials = jnp.concatenate([gate_partial, up_partial], 0)
    paired_factors = jnp.concatenate([a_gate, a_up], 0)
    gradient_rows_out = (
        contract_pair(gate_gradient, gate_weight, 0, 0)
        + contract_pair(up_gradient, up_weight, 0, 0)
        + ADAPTER_SCALE * contract_pair(paired_partials, paired_factors, 0, 0)
    )
    shared_slice = (
        ADAPTER_SCALE * contract_pair(gate_partial, input_rows, 1, 0),
        ADAPTER_SCALE * contract_pair(up_partial, input_rows, 1, 0),
        ADAPTER_SCALE * contract_pair(output_gradient_rows, down_partial, 0, 1),
    )
    owned_slice = (
        ADAPTER_SCALE * contract_pair(gate_gradient, gate_projected_lower, 1, 1),
        ADAPTER_SCALE * contract_pair(up_gradient, up_projected_lower, 1, 1),
        ADAPTER_SCALE * contract_pair(down_projected_lower, hidden_units, 1, 1),
    )
    return (gradient_rows_out, shared_slice, owned_slice)


def rows_backward_parts(input_rows, output_gradient_rows, params):
    (
        gate_weight,
        up_weight,
        down_weight,
        a_gate,
        gate_adapter_upper,
        a_up,
        up_adapter_upper,
        down_adapter_lower,
        b_down,
    ) = params
    gate_projected_lower = contract_pair(a_gate, input_rows, 1, 1).astype(jnp.bfloat16)
    up_projected_lower = contract_pair(a_up, input_rows, 1, 1).astype(jnp.bfloat16)
    gate_preactivation = contract_pair(
        gate_weight, input_rows, 1, 1
    ) + ADAPTER_SCALE * contract_pair(gate_adapter_upper, gate_projected_lower, 1, 0)
    up_preactivation = contract_pair(up_weight, input_rows, 1, 1) + ADAPTER_SCALE * contract_pair(
        up_adapter_upper, up_projected_lower, 1, 0
    )
    sigmoid_gate = jax.nn.sigmoid(gate_preactivation)
    silu_gate = gate_preactivation * sigmoid_gate
    hidden_units = (silu_gate * up_preactivation).astype(jnp.bfloat16)
    down_projected_lower = contract_pair(b_down, output_gradient_rows, 0, 1).astype(jnp.bfloat16)
    hidden_gradient = contract_pair(
        down_weight, output_gradient_rows, 1, 1
    ) + ADAPTER_SCALE * contract_pair(down_adapter_lower, down_projected_lower, 0, 0)
    gate_gradient = (
        hidden_gradient
        * up_preactivation
        * sigmoid_gate
        * (1.0 + gate_preactivation * (1.0 - sigmoid_gate))
    ).astype(jnp.bfloat16)
    up_gradient = (hidden_gradient * silu_gate).astype(jnp.bfloat16)
    gate_partial = contract_pair(gate_gradient, gate_adapter_upper, 0, 0).astype(jnp.bfloat16)
    up_partial = contract_pair(up_gradient, up_adapter_upper, 0, 0).astype(jnp.bfloat16)
    down_partial = contract_pair(hidden_units, down_adapter_lower, 0, 1).astype(jnp.bfloat16)
    paired_partials = jnp.concatenate([gate_partial, up_partial], 1)
    paired_factors = jnp.concatenate([a_gate, a_up], 0)
    gradient_rows_out = (
        contract_pair(gate_gradient, gate_weight, 0, 0)
        + contract_pair(up_gradient, up_weight, 0, 0)
        + ADAPTER_SCALE * contract_pair(paired_partials, paired_factors, 1, 0)
    )
    parts = jnp.concatenate([gate_partial, up_partial, down_partial], 1)
    owned_slice = (
        ADAPTER_SCALE * contract_pair(gate_gradient, gate_projected_lower, 1, 1),
        ADAPTER_SCALE * contract_pair(up_gradient, up_projected_lower, 1, 1),
        ADAPTER_SCALE * contract_pair(down_projected_lower, hidden_units, 1, 1),
    )
    return (gradient_rows_out, parts, owned_slice)


def local(
    tokens,
    output_gradient,
    routing,
    router_gate_values,
    gate_weight,
    up_weight,
    down_weight,
    adapter_lower_gate,
    adapter_upper_gate,
    adapter_lower_up,
    adapter_upper_up,
    adapter_lower_down,
    adapter_upper_down,
):
    experts = lax.axis_size("expert")
    shards = lax.axis_size("dp")
    tok_local, feat_local = tokens.shape
    choose = routing.shape[1]
    complete_width = feat_local * experts
    capacity = min(tok_local, 6 * tok_local // experts)
    adapter_rank = adapter_lower_gate.shape[1]
    chunks = NUM_CHUNKS
    piece = capacity // chunks
    params = (
        gate_weight[0],
        up_weight[0],
        down_weight[0],
        adapter_lower_gate[0],
        adapter_upper_gate[0],
        adapter_lower_up[0],
        adapter_upper_up[0],
        adapter_lower_down[0],
        adapter_upper_down[0],
    )
    positions = slot_numbers(routing, experts)
    zero_row = jnp.zeros((1, feat_local), jnp.bfloat16)
    source, member = slot_sources(routing, positions, experts, capacity)
    clamped = jnp.minimum(source, tok_local - 1)
    slot_gate = jnp.where(
        source < tok_local, router_gate_values.reshape(-1)[clamped * choose + member], 0.0
    )
    send_x = jnp.concatenate([tokens, zero_row], 0)[source].reshape(experts, capacity, feat_local)
    send_dy = (
        (
            slot_gate[:, None]
            * jnp.concatenate([output_gradient, zero_row], 0)[source].astype(jnp.float32)
        )
        .astype(jnp.bfloat16)
        .reshape(experts, capacity, feat_local)
    )
    send_both = jnp.concatenate([send_x, send_dy], axis=2)
    recv_both = lax.all_to_all(send_both, "expert", split_axis=0, concat_axis=2, tiled=True)[0]
    recv_both = recv_both.reshape(capacity, experts, 2, feat_local).transpose(0, 2, 1, 3)
    recv_both = recv_both.reshape(capacity, 2 * complete_width)
    rows_chunks = []
    part_chunks = []
    x_chunks = []
    dy_chunks = []
    owned_total = None
    for c in range(chunks):
        part = recv_both[c * piece : (c + 1) * piece]
        gathered = lax.all_gather(part, "dp", axis=0, tiled=True)
        x_rows = gathered[:, :complete_width]
        dy_rows = gathered[:, complete_width:]
        rows_out, parts, owned_slice = rows_backward_parts(x_rows, dy_rows, params)
        if c == 0:
            owned_total = owned_slice
        else:
            owned_total = jax.tree.map(jnp.add, owned_total, owned_slice)
        rows_chunks.append(rows_out.astype(jnp.bfloat16).reshape(shards, piece, complete_width))
        part_chunks.append(parts.reshape(shards, piece, 3 * adapter_rank))
        x_chunks.append(x_rows.reshape(shards, piece, complete_width))
        dy_chunks.append(dy_rows.reshape(shards, piece, complete_width))
    rows_all = jnp.concatenate(rows_chunks, 1)
    parts_all = jnp.concatenate(part_chunks, 1)
    parts_all = jnp.pad(parts_all, ((0, 0), (0, 0), (0, PART_COLS - 3 * adapter_rank)))
    packed = jnp.concatenate([rows_all, parts_all], 2)
    summed_packed = lax.psum_scatter(packed, "dp", scatter_dimension=0, tiled=True)[0]
    summed = summed_packed[:, :complete_width]
    parts_mine = summed_packed[:, complete_width : complete_width + 3 * adapter_rank]
    parts_sum = lax.all_gather(parts_mine, "dp", axis=0, tiled=True)
    parts_sum = parts_sum.reshape(shards, capacity, 3 * adapter_rank)
    x_all = jnp.concatenate(x_chunks, 1).reshape(shards * capacity, complete_width)
    dy_all = jnp.concatenate(dy_chunks, 1).reshape(shards * capacity, complete_width)
    parts_sum = parts_sum.reshape(shards * capacity, 3 * adapter_rank)
    grad_a_gate = ADAPTER_SCALE * contract_pair(parts_sum[:, :adapter_rank], x_all, 0, 0)
    grad_a_up = ADAPTER_SCALE * contract_pair(
        parts_sum[:, adapter_rank : 2 * adapter_rank], x_all, 0, 0
    )
    grad_b_down = ADAPTER_SCALE * contract_pair(dy_all, parts_sum[:, 2 * adapter_rank :], 0, 0)
    returned_rows = lax.all_to_all(
        summed.reshape(capacity, experts, feat_local),
        "expert",
        split_axis=1,
        concat_axis=1,
        tiled=True,
    ).astype(jnp.float32)
    lookup = positions * experts + routing
    grad_x = jnp.sum(returned_rows.reshape(capacity * experts, feat_local)[lookup], axis=1).astype(
        jnp.bfloat16
    )
    return (
        grad_x,
        grad_a_gate[None],
        owned_total[0][None],
        grad_a_up[None],
        owned_total[1][None],
        owned_total[2][None],
        grad_b_down[None],
    )


def solution(mesh):
    return jax.shard_map(
        local,
        mesh=mesh,
        in_specs=(
            P("dp", "expert"),
            P("dp", "expert"),
            P("dp", None),
            P("dp", None),
            P("expert", "dp", None),
            P("expert", "dp", None),
            P("expert", "dp", None),
            P("expert", None, None),
            P("expert", "dp", None),
            P("expert", None, None),
            P("expert", "dp", None),
            P("expert", None, "dp"),
            P("expert", None, None),
        ),
        out_specs=(
            P("dp", "expert"),
            P("expert", None, None),
            P("expert", "dp", None),
            P("expert", None, None),
            P("expert", "dp", None),
            P("expert", None, "dp"),
            P("expert", None, None),
        ),
        check_vma=False,
    )
```

profile of v0, /device:TPU:1, one launch (start us, length us, event | category | flops | bytes accessed | tf_op | source)
XLA Modules:
  0.0 469.6 jit_solution(13800577406468424391)
XLA Ops:
  14.1 5.0 %gather_fusion.1 = f32[768]{0:T(1024)S(1)} fusion(f32[256]{0:T(256)S(1)} %reshape.120, s32[1024]{0:T(1024)S(1)} %get-tuple-element.23), kind=kCustom, calls=%fused_computation.1 | custom fusion | bytes 9216 | tf_op jit(solution)/shard_map/gather | solution.py:186
  19.2 2.7 gather_fusion.2
  21.9 2.7 gather_fusion
  25.1 27.4 %all_to_all.20 = bf16[8,96,1024]{2,1,0:T(8,128)(2,1)S(1)} all-to-all(bf16[8,96,1024]{2,1,0:T(8,128)(2,1)S(1)} %pad_maximum_fusion.3), channel_id=1, replica_groups=mesh['dp'=16,'expert'=8] {'expert'}, dimensions={0} | all-to-all | bytes 3145728 | tf_op jit(solution)/shard_map/all_to_all | solution.py:198
  60.3 87.8 %all-gather.4.cloned.1.call-done = bf16[768,8192]{1,0:T(8,128)(2,1)} async-done(((bf16[48,8192]{1,0:T(8,128)(2,1)}), bf16[768,8192]{1,0:T(8,128)(2,1)}) %all-gather.4.cloned.1.call-update) | async-done | bytes 12582928 | tf_op jit(solution)/shard_map/all_gather | solution.py:208
  148.2 4.7 convolution_convert_fusion.11
  152.9 6.0 %fusion.21 = f32[768,448]{0,1:T(8,128)S(1)} fusion(bf16[1,448,4096]{2,1,0:T(8,128)(2,1)S(1)} %copy-done.29, bf16[768,8192]{1,0:T(8,128)(2,1)} %all-gather.4.cloned.1.call-done), kind=kOutput, calls=%fused_computation.35 | convolution fusion | flops 2818572288 | bytes 11337728 | tf_op jit(solution)/shard_map/dot_general | solution.py:12
  161.7 3.1 fusion.17
  167.3 3.3 fusion.9
  172.9 6.4 %fusion.15 = f32[768,4096]{1,0:T(8,128)} fusion(bf16[448,768]{1,0:T(8,128)(2,1)S(1)} %get-tuple-element.13, bf16[1,448,4096]{2,1,0:T(8,128)(2,1)S(1)} %copy-done.3), kind=kOutput, calls=%fused_computation.29 | convolution fusion | flops 2818572288 | bytes 16941056 | tf_op jit(solution)/shard_map/dot_general | solution.py:12
  179.3 6.3 %fusion.7 = f32[768,4096]{1,0:T(8,128)} fusion(bf16[448,768]{1,0:T(8,128)(2,1)S(1)} %get-tuple-element.11, bf16[1,448,4096]{2,1,0:T(8,128)(2,1)S(1)} %copy-done.5), kind=kOutput, calls=%fused_computation.21 | convolution fusion | flops 2818572288 | bytes 16941056 | tf_op jit(solution)/shard_map/dot_general | solution.py:12
  185.6 54.4 %all-gather.6.cloned.1.call-done = bf16[768,8192]{1,0:T(8,128)(2,1)} async-done(((bf16[48,8192]{1,0:T(8,128)(2,1)}), bf16[768,8192]{1,0:T(8,128)(2,1)}) %all-gather.6.cloned.1.call-update) | async-done | bytes 12582928 | tf_op jit(solution)/shard_map/all_gather | solution.py:208
  240.0 4.7 convolution_convert_fusion.8
  244.7 6.0 %fusion.19 = f32[768,448]{0,1:T(8,128)S(1)} fusion(bf16[1,448,4096]{2,1,0:T(8,128)(2,1)S(1)} %copy-done.30, bf16[768,8192]{1,0:T(8,128)(2,1)} %all-gather.6.cloned.1.call-done), kind=kOutput, calls=%fused_computation.33 | convolution fusion | flops 2818572288 | bytes 11337728 | tf_op jit(solution)/shard_map/dot_general | solution.py:12
  253.1 3.1 fusion.13
  258.7 3.5 fusion.5
  263.3 6.3 %fusion.11 = f32[768,4096]{1,0:T(8,128)} fusion(bf16[448,768]{1,0:T(8,128)(2,1)S(1)} %get-tuple-element.16, bf16[1,448,4096]{2,1,0:T(8,128)(2,1)S(1)} %copy-done.4), kind=kOutput, calls=%fused_computation.25 | convolution fusion | flops 2818572288 | bytes 16941056 | tf_op jit(solution)/shard_map/dot_general | solution.py:12
  269.9 6.3 %fusion.3 = f32[768,4096]{1,0:T(8,128)} fusion(bf16[448,768]{1,0:T(8,128)(2,1)S(1)} %get-tuple-element.14, bf16[1,448,4096]{2,1,0:T(8,128)(2,1)S(1)} %copy-done.6), kind=kOutput, calls=%fused_computation.17 | convolution fusion | flops 2818572288 | bytes 16941056 | tf_op jit(solution)/shard_map/dot_general | solution.py:12
  278.3 9.3 %add_convert_fusion.1 = bf16[768,4096]{1,0:T(8,128)(2,1)S(1)} fusion(f32[768,4096]{1,0:T(8,128)} %fusion.7, f32[768,4096]{1,0:T(8,128)} %fusion.15, bf16[16,4096]{1,0:T(8,128)(2,1)S(1)} %bitcast.196, bf16[16,4096]{1,0:T(8,128)(2,1)S(1)} %bitcast.198, bf16[768,16]{0,1:T(8,128)(2,1)} %copy-done.13, bf16[768,16]{0,1:T(8,128)(2,1)} %copy-done.12), kind=kOutput, calls=%fused_computation.10 | convolution fusion | flops 214532096 | bytes 31768576 | tf_op jit(solution)/shard_map/dot_general | solution.py:12
  287.5 12.0 %add_convert_fusion = bf16[768,4096]{1,0:T(8,128)(2,1)} fusion(f32[768,4096]{1,0:T(8,128)} %fusion.3, f32[768,4096]{1,0:T(8,128)} %fusion.11, bf16[16,4096]{1,0:T(8,128)(2,1)S(1)} %bitcast.197, bf16[16,4096]{1,0:T(8,128)(2,1)S(1)} %bitcast.199, bf16[768,16]{0,1:T(8,128)(2,1)S(1)} %convolution_convert_fusion.2, bf16[768,16]{0,1:T(8,128)(2,1)S(1)} %convolution_convert_fusion.3), kind=kOutput, calls=%fused_computation.9 | convolution fusion | flops 214532096 | bytes 31768576 | tf_op jit(solution)/shard_map/dot_general | solution.py:12
  299.5 10.4 %pad_maximum_fusion = bf16[16,96,4224]{2,1,0:T(8,128)(2,1)} fusion(bf16[16,96,128]{2,1,0:T(8,128)(2,1)S(1)} %fusion.46, bf16[16,48,4096]{2,1,0:T(8,128)(2,1)} %bitcast.176, bf16[16,48,4096]{2,1,0:T(8,128)(2,1)S(1)} %bitcast.172), kind=kLoop, calls=%fused_computation.6 | loop fusion | flops 38928384 | bytes 25952256 | tf_op jit(solution)/shard_map/concatenate | solution.py:223
  316.6 5.9 %fusion.93 = (bf16[768,4096]{1,0:T(8,128)(2,1)S(1)}, bf16[768,4096]{1,0:T(8,128)(2,1)S(1)}) fusion(bf16[768,8192]{1,0:T(8,128)(2,1)} %all-gather.6.cloned.1.call-done), kind=kLoop, calls=%fused_computation.158 | loop fusion | bytes 25165824 | tf_op jit(solution)/shard_map/slice | solution.py:210
  322.5 5.7 %fusion.92 = (bf16[768,4096]{1,0:T(8,128)(2,1)S(1)}, bf16[768,4096]{1,0:T(8,128)(2,1)S(1)}) fusion(bf16[768,8192]{1,0:T(8,128)(2,1)} %all-gather.4.cloned.1.call-done), kind=kLoop, calls=%fused_computation.157 | loop fusion | bytes 25165824 | tf_op jit(solution)/shard_map/slice | solution.py:210
  328.2 8.7 %pad_maximum_fusion.2 = bf16[16,96,4096]{2,1,0:T(8,128)(2,1)} fusion(bf16[16,48,4096]{2,1,0:T(8,128)(2,1)S(1)} %bitcast.174, bf16[16,48,4096]{2,1,0:T(8,128)(2,1)S(1)} %bitcast.177), kind=kLoop, calls=%fused_computation.8 | loop fusion | flops 25165824 | bytes 25165824 | tf_op jit(solution)/shard_map/concatenate | solution.py:230
  336.9 8.6 %pad_maximum_fusion.1 = bf16[16,96,4096]{2,1,0:T(8,128)(2,1)} fusion(bf16[16,48,4096]{2,1,0:T(8,128)(2,1)S(1)} %bitcast.173, bf16[16,48,4096]{2,1,0:T(8,128)(2,1)S(1)} %bitcast.175), kind=kLoop, calls=%fused_computation.7 | loop fusion | flops 25165824 | bytes 25165824 | tf_op jit(solution)/shard_map/concatenate | solution.py:229
  345.5 60.0 %reduce-scatter.4.cloned.1.call-done = bf16[1,96,4224]{2,1,0:T(8,128)(2,1)} async-done(((bf16[16,96,4224]{2,1,0:T(8,128)(2,1)}), bf16[1,96,4224]{2,1,0:T(8,128)(2,1)}) %reduce-scatter.4.cloned.1.call-update) | async-done | bytes 811024
  407.5 16.7 %all-gather = bf16[16,96,48]{1,2,0:T(8,128)(2,1)S(1)} all-gather(bf16[1,96,48]{1,2,0:T(8,128)(2,1)S(1)} %copy.88), channel_id=1, replica_groups=mesh['dp'=16,'expert'=8] {'dp'}, dimensions={0}, use_global_device_ids=true | all-gather | bytes 156672 | tf_op jit(solution)/shard_map/all_gather | solution.py:227
  424.5 7.2 %fusion.1 = f32[1,16,4096]{2,1,0:T(8,128)} fusion(bf16[1536,4096]{1,0:T(8,128)(2,1)} %bitcast.169, bf16[1536,48]{0,1:T(8,128)(2,1)S(1)} %reshape.191), kind=kOutput, calls=%fused_computation.14 | convolution fusion | flops 201392128 | bytes 12894208 | tf_op jit(solution)/shard_map/dot_general | solution.py:12
  432.7 2.4 fusion.2
  436.2 11.4 %all-to-all-start.1 = ((bf16[96,8,512]{2,0,1:T(8,128)(2,1)}), bf16[96,8,512]{2,0,1:T(8,128)(2,1)S(1)}, u32[]{:S(2)}, u32[]{:S(2)}) async-start(bf16[96,8,512]{2,0,1:T(8,128)(2,1)} %bitcast.166), calls=%async_computation.1 | async-start | bytes 1572864 | tf_op jit(solution)/shard_map/all_to_all | solution.py:237
  447.6 7.0 %fusion = f32[1,4096,16]{1,2,0:T(8,128)} fusion(bf16[1536,4096]{1,0:T(8,128)(2,1)} %bitcast.171, bf16[1536,48]{0,1:T(8,128)(2,1)S(1)} %reshape.191), kind=kOutput, calls=%fused_computation.12 | convolution fusion | flops 201392128 | bytes 12894208 | tf_op jit(solution)/shard_map/dot_general | solution.py:12
  454.6 5.3 %all-to-all-done.1 = bf16[96,8,512]{2,0,1:T(8,128)(2,1)S(1)} async-done(((bf16[96,8,512]{2,0,1:T(8,128)(2,1)}), bf16[96,8,512]{2,0,1:T(8,128)(2,1)S(1)}, u32[]{:S(2)}, u32[]{:S(2)}) %all-to-all-start.1) | async-done | bytes 786464 | tf_op jit(solution)/shard_map/all_to_all | solution.py:237
  (155 shorter events, 45.0 us)
Async XLA Ops:
  7.2 141.0 %copy-start = (bf16[1,4096,16]{1,2,0:T(8,128)(2,1)S(1)}, bf16[1,4096,16]{1,2,0:T(8,128)(2,1)}, u32[]{:S(2)}) copy-start(bf16[1,4096,16]{1,2,0:T(8,128)(2,1)} %param.25) | copy-start | bytes 393220
  7.2 12.0 %copy-start.14 = (bf16[128,512]{1,0:T(8,128)(2,1)S(1)}, bf16[128,512]{1,0:T(8,128)(2,1)}, u32[]{:S(2)}) copy-start(bf16[128,512]{1,0:T(8,128)(2,1)} %param.13) | copy-start | bytes 393220
  7.2 12.0 %copy-start.15 = (bf16[128,512]{1,0:T(8,128)(2,1)S(1)}, bf16[128,512]{1,0:T(8,128)(2,1)}, u32[]{:S(2)}) copy-start(bf16[128,512]{1,0:T(8,128)(2,1)} %param.14) | copy-start | bytes 393220
  7.2 141.0 %all-gather.4.cloned.1.call-start = ((), (), s32[]{:S(2)}) async-start(), calls=%async_computation.3 | async-start | bytes 13369344 | tf_op jit(solution)/shard_map/all_gather | solution.py:208
  58.3 181.7 %all-gather.6.cloned.1.call-start = ((), (), s32[]{:S(2)}) async-start(), calls=%async_computation.4 | async-start | bytes 13369344 | tf_op jit(solution)/shard_map/all_gather | solution.py:208
  59.8 345.7 %reduce-scatter.4.cloned.1.call-start = ((), (), s32[]{:S(2)}) async-start(), calls=%async_computation.5 | async-start | bytes 13787136
  148.2 4.7 copy-start.29
  148.2 11.1 %slice-start = ((s8[12582912]{0:T(1024)(128)(4,1)}), s8[4194304]{0:T(1024)(128)(4,1)S(1)}, s32[]{:S(2)}) async-start(s8[12582912]{0:T(1024)(128)(4,1)} %bitcast.179), calls=%async_computation.6 | async-start | bytes 8388608
  152.8 6.0 %copy-start.18 = (bf16[768,16]{0,1:T(8,128)(2,1)}, bf16[768,16]{0,1:T(8,128)(2,1)S(1)}, u32[]{:S(2)}) copy-start(bf16[768,16]{0,1:T(8,128)(2,1)S(1)} %convolution_convert_fusion.11) | copy-start | bytes 73732
  152.8 6.0 %copy-start.11 = (bf16[1,16,448]{2,1,0:T(8,128)(2,1)S(1)}, bf16[1,16,448]{2,1,0:T(8,128)(2,1)}, u32[]{:S(2)}) copy-start(bf16[1,16,448]{2,1,0:T(8,128)(2,1)} %param.24) | copy-start | bytes 43012
  152.9 6.4 %slice-start.1 = ((s8[12582912]{0:T(1024)(128)(4,1)}), s8[4194304]{0:T(1024)(128)(4,1)S(1)}, s32[]{:S(2)}) async-start(s8[12582912]{0:T(1024)(128)(4,1)} %bitcast.179), calls=%async_computation.7 | async-start | bytes 8388608
  152.9 6.4 %slice-start.2 = ((s8[12582912]{0:T(1024)(128)(4,1)}), s8[4194304]{0:T(1024)(128)(4,1)S(1)}, s32[]{:S(2)}) async-start(s8[12582912]{0:T(1024)(128)(4,1)} %bitcast.179), calls=%async_computation.8 | async-start | bytes 8388608
  152.9 6.4 %copy-start.8 = (bf16[1,16,4096]{2,1,0:T(8,128)(2,1)S(1)}, bf16[1,16,4096]{2,1,0:T(8,128)(2,1)}, u32[]{:S(2)}) copy-start(bf16[1,16,4096]{2,1,0:T(8,128)(2,1)} %param.22) | copy-start | bytes 393220
  161.7 3.1 copy-start.10
  161.7 3.5 copy-start.9
  167.3 3.3 copy-start.25
  167.3 3.3 copy-start.24
  172.7 105.2 %copy-start.12 = (bf16[768,16]{0,1:T(8,128)(2,1)}, bf16[768,16]{0,1:T(8,128)(2,1)S(1)}, u32[]{:S(2)}) copy-start(bf16[768,16]{0,1:T(8,128)(2,1)S(1)} %convolution_convert_fusion.5) | copy-start | bytes 73732
  172.9 105.0 %copy-start.13 = (bf16[768,16]{0,1:T(8,128)(2,1)}, bf16[768,16]{0,1:T(8,128)(2,1)S(1)}, u32[]{:S(2)}) copy-start(bf16[768,16]{0,1:T(8,128)(2,1)S(1)} %convolution_convert_fusion.4) | copy-start | bytes 73732
  240.0 4.7 copy-start.30
  240.0 11.1 %slice-start.3 = ((s8[12582912]{0:T(1024)(128)(4,1)}), s8[4194304]{0:T(1024)(128)(4,1)S(1)}, s32[]{:S(2)}) async-start(s8[12582912]{0:T(1024)(128)(4,1)} %bitcast.181), calls=%async_computation.9 | async-start | bytes 8388608
  244.6 6.0 %copy-start.22 = (bf16[768,16]{0,1:T(8,128)(2,1)}, bf16[768,16]{0,1:T(8,128)(2,1)S(1)}, u32[]{:S(2)}) copy-start(bf16[768,16]{0,1:T(8,128)(2,1)S(1)} %convolution_convert_fusion.8) | copy-start | bytes 73732
  244.6 6.4 %slice-start.4 = ((s8[12582912]{0:T(1024)(128)(4,1)}), s8[4194304]{0:T(1024)(128)(4,1)S(1)}, s32[]{:S(2)}) async-start(s8[12582912]{0:T(1024)(128)(4,1)} %bitcast.181), calls=%async_computation.10 | async-start | bytes 8388608
  244.7 6.4 %slice-start.5 = ((s8[12582912]{0:T(1024)(128)(4,1)}), s8[4194304]{0:T(1024)(128)(4,1)S(1)}, s32[]{:S(2)}) async-start(s8[12582912]{0:T(1024)(128)(4,1)} %bitcast.181), calls=%async_computation.11 | async-start | bytes 8388608
  258.7 3.5 copy-start.27
  263.1 13.1 %copy-start.7 = (bf16[448,768]{1,0:T(8,128)(2,1)}, bf16[448,768]{1,0:T(8,128)(2,1)S(1)}, u32[]{:S(2)}) copy-start(bf16[448,768]{1,0:T(8,128)(2,1)S(1)} %get-tuple-element.15) | copy-start | bytes 2064388
  309.9 4.2 copy-start.26
  309.9 4.5 copy-start.28
  309.9 5.4 %copy-start.17 = (bf16[768,16]{0,1:T(8,128)(2,1)S(1)}, bf16[768,16]{0,1:T(8,128)(2,1)}, u32[]{:S(2)}) copy-start(bf16[768,16]{0,1:T(8,128)(2,1)} %copy-done.16) | copy-start | bytes 73732
  310.0 5.7 %copy-start.21 = (bf16[768,16]{0,1:T(8,128)(2,1)S(1)}, bf16[768,16]{0,1:T(8,128)(2,1)}, u32[]{:S(2)}) copy-start(bf16[768,16]{0,1:T(8,128)(2,1)} %copy-done.20) | copy-start | bytes 73732
  424.5 8.3 %copy-start.2 = (bf16[16,96,4096]{2,1,0:T(8,128)(2,1)S(1)}, bf16[16,96,4096]{2,1,0:T(8,128)(2,1)}, u32[]{:S(2)}) copy-start(bf16[16,96,4096]{2,1,0:T(8,128)(2,1)} %pad_maximum_fusion.1) | copy-start | bytes 37748740
  436.2 23.7 %all-to-all-start.1 = ((bf16[96,8,512]{2,0,1:T(8,128)(2,1)}), bf16[96,8,512]{2,0,1:T(8,128)(2,1)S(1)}, u32[]{:S(2)}, u32[]{:S(2)}) async-start(bf16[96,8,512]{2,0,1:T(8,128)(2,1)} %bitcast.166), calls=%async_computation.1 | async-start | bytes 1572864 | tf_op jit(solution)/shard_map/all_to_all | solution.py:237
  (9 other events, 20.6 us)
Sparse Core Ops, SparseCore 0:
  58.4 89.7 all-gather.3
  150.3 89.5 all-gather.5
  310.1 95.3 reduce-scatter.3
where the time goes:
time: 477 us; the launch traced here: 470 us
  waiting for transfers between devices  207 us (43%)
  matrix products  117 us (25%)
  blocking collectives  44.1 us (9%)
  local copies, waits for them, and re-layouts  42.5 us (9%)
  other arithmetic  32 us (7%)
  between operations  14.6 us (3%)
  starting transfers between devices  12 us (3%)
    all_gather x2, waiting for transfers between devices, local(): gathered = lax.all_gather(part, 'dp', axis=0, tiled=True)  142 us
    dot_general x39, matrix products, contract_pair(): lax.dot_general(left, right, (((left_axis,), (right_axis,)), ((), ())), p...  117 us
    unnamed x4, waiting for transfers between devices  60 us
    all_to_all x1, blocking collectives, local(): lax.all_to_all(send_both, 'expert', split_axis=0, concat_axis=2, tiled=True)  27.4 us
    all_gather x1, blocking collectives, local(): parts_sum = lax.all_gather(parts_mine, 'dp', axis=0, tiled=True)  16.7 us
    slice x2, local copies, waits for them, and re-layouts, local(): dy_rows = gathered[:, complete_width:]  11.6 us
    all_to_all x1, starting transfers between devices, local(): lax.all_to_all(summed.reshape(capacity, experts, feat_local), 'expert', s...  11.4 us
    concatenate x1, other arithmetic, local(): packed = jnp.concatenate([rows_all, parts_all], 2)  10.4 us
  transfers between devices with their start and end apart: 4, of which 4 were waited for; matrix products, arithmetic and copies ran while one was open for 17% of the time, Pallas kernels for 0%

commit v1 on v0

--- a/solution.py
+++ b/solution.py
@@ -6,6 +6,13 @@
 ADAPTER_SCALE = 2.0
 NUM_CHUNKS = 2
 PART_COLS = 128
+
+
+def all_by_exchange(array, name, dim):
+    peers = lax.axis_size(name)
+    blocks = jnp.stack([array for _ in range(peers)])
+    blocks = lax.all_to_all(blocks, name, split_axis=0, concat_axis=0)
+    return jnp.concatenate(blocks, axis=dim)
 
 
 def contract_pair(left, right, left_axis, right_axis):
@@ -205,7 +212,7 @@
     owned_total = None
     for c in range(chunks):
         part = recv_both[c * piece : (c + 1) * piece]
-        gathered = lax.all_gather(part, "dp", axis=0, tiled=True)
+        gathered = all_by_exchange(part, "dp", 0)
         x_rows = gathered[:, :complete_width]
         dy_rows = gathered[:, complete_width:]
         rows_out, parts, owned_slice = rows_backward_parts(x_rows, dy_rows, params)

time: 477 us -> 818 us (1.71)
  waiting for transfers between devices: 207 us -> 494 us
  matrix products: 117 us -> 139 us
  starting transfers between devices: 12 us -> 30.9 us
  local copies, waits for them, and re-layouts: 42.5 us -> 52.7 us
    all_to_all x0 -> x2, waiting for transfers between devices: none -> 417 us  [all_by_exchange(): blocks = lax.all_to_all(blocks, name, split_axis=0, concat_axis=0)]
    all_gather x2 -> x0, waiting for transfers between devices: 142 us -> none  [local(): gathered = lax.all_gather(part, 'dp', axis=0, tiled=True)]
    dot_general x39, matrix products: 117 us -> 139 us  [contract_pair(): lax.dot_general(left, right, (((left_axis,), (right_axis,)), ((), ())), p...]
    all_to_all x0 -> x2, starting transfers between devices: none -> 19.2 us  [all_by_exchange(): blocks = lax.all_to_all(blocks, name, split_axis=0, concat_axis=0)]
    another operation x0 -> x2, local copies, waits for them, and re-layouts: none -> 12.2 us  [all_by_exchange(): blocks = jnp.stack([array for _ in range(peers)])]
    unnamed x4 -> x2, waiting for transfers between devices: 60 us -> 72 us
  transfers between devices with their start and end apart: 4 -> 4, of which waited for: 4 -> 4; matrix products, arithmetic and copies ran while one was open for 17% -> 6% of each run, Pallas kernels for 0% -> 0%
where the time goes in v1:
time: 818 us; the launch traced here: 808 us
  waiting for transfers between devices  494 us (60%)
  matrix products  139 us (17%)
  local copies, waits for them, and re-layouts  52.7 us (6%)
  blocking collectives  43.9 us (5%)
  other arithmetic  32.1 us (4%)
  starting transfers between devices  30.9 us (4%)
  between operations  15.1 us (2%)
    all_to_all x2, waiting for transfers between devices, all_by_exchange(): blocks = lax.all_to_all(blocks, name, split_axis=0, concat_axis=0)  417 us
    dot_general x39, matrix products, contract_pair(): lax.dot_general(left, right, (((left_axis,), (right_axis,)), ((), ())), p...  139 us
    unnamed x2, waiting for transfers between devices  72 us
    all_to_all x1, blocking collectives, local(): lax.all_to_all(send_both, 'expert', split_axis=0, concat_axis=2, tiled=True)  27.4 us
    all_to_all x2, starting transfers between devices, all_by_exchange(): blocks = lax.all_to_all(blocks, name, split_axis=0, concat_axis=0)  19.2 us
    all_gather x1, blocking collectives, local(): parts_sum = lax.all_gather(parts_mine, 'dp', axis=0, tiled=True)  16.5 us
  transfers between devices with their start and end apart: 4, of which 4 were waited for; matrix products, arithmetic and copies ran while one was open for 6% of the time, Pallas kernels for 0%

profile of v1, /device:TPU:1, one launch (start us, length us, event | category | flops | bytes accessed | tf_op | source)
XLA Modules:
  0.0 808.1 jit_solution(10096176300103558296)
XLA Ops:
  14.0 5.0 gather_fusion.1
  26.7 27.4 %all_to_all.30 = bf16[8,96,1024]{2,1,0:T(8,128)(2,1)S(1)} all-to-all(bf16[8,96,1024]{2,1,0:T(8,128)(2,1)S(1)} %pad_maximum_fusion.3), channel_id=1, replica_groups=mesh['dp'=16,'expert'=8] {'expert'}, dimensions={0} | all-to-all | bytes 3145728 | tf_op jit(solution)/shard_map/all_to_all | solution.py:205
  59.0 6.1 stack.11
  65.1 6.8 all-to-all-start.2
  72.5 218.9 %all-to-all-done.2 = bf16[16,48,8192]{2,1,0:T(8,128)(2,1)} async-done(((bf16[16,48,8192]{2,1,0:T(8,128)(2,1)}), bf16[16,48,8192]{2,1,0:T(8,128)(2,1)}, u32[]{:S(2)}, u32[]{:S(2)}) %all-to-all-start.2) | async-done | bytes 12582944 | tf_op jit(solution)/shard_map/all_to_all | solution.py:14
  291.3 6.2 stack.9
  297.5 12.4 %all-to-all-start.1 = ((bf16[16,48,8192]{2,1,0:T(8,128)(2,1)}), bf16[16,48,8192]{2,1,0:T(8,128)(2,1)}, u32[]{:S(2)}, u32[]{:S(2)}) async-start(bf16[16,48,8192]{2,1,0:T(8,128)(2,1)} %stack.9), calls=%async_computation.1 | async-start | bytes 25165824 | tf_op jit(solution)/shard_map/all_to_all | solution.py:14
  319.3 198.0 %all-to-all-done.1 = bf16[16,48,8192]{2,1,0:T(8,128)(2,1)} async-done(((bf16[16,48,8192]{2,1,0:T(8,128)(2,1)}), bf16[16,48,8192]{2,1,0:T(8,128)(2,1)}, u32[]{:S(2)}, u32[]{:S(2)}) %all-to-all-start.1) | async-done | bytes 12582944 | tf_op jit(solution)/shard_map/all_to_all | solution.py:14
  530.9 4.7 convolution_convert_fusion.11
  535.5 5.8 fusion.5
  541.4 6.5 fusion.9
  547.9 5.8 fusion.19
  553.7 6.0 fusion.21
  559.7 5.8 fusion.13
  565.6 5.8 fusion.17
  574.6 6.4 fusion.15
  581.1 6.4 fusion.7
  589.6 6.4 fusion.11
  596.2 6.4 fusion.3
  604.6 9.2 %add_convert_fusion.1 = bf16[768,4096]{1,0:T(8,128)(2,1)S(1)} fusion(f32[768,4096]{1,0:T(8,128)} %fusion.7, f32[768,4096]{1,0:T(8,128)} %fusion.15, bf16[16,4096]{1,0:T(8,128)(2,1)S(1)} %bitcast.194, bf16[16,4096]{1,0:T(8,128)(2,1)S(1)} %bitcast.196, bf16[768,16]{0,1:T(8,128)(2,1)S(1)} %convolution_convert_fusion.4, bf16[768,16]{0,1:T(8,128)(2,1)} %copy-done.10), kind=kOutput, calls=%fused_computation.10 | convolution fusion | flops 214532096 | bytes 31768576 | tf_op jit(solution)/shard_map/dot_general | solution.py:19
  613.9 12.0 %add_convert_fusion = bf16[768,4096]{1,0:T(8,128)(2,1)} fusion(f32[768,4096]{1,0:T(8,128)} %fusion.3, f32[768,4096]{1,0:T(8,128)} %fusion.11, bf16[16,4096]{1,0:T(8,128)(2,1)S(1)} %bitcast.195, bf16[16,4096]{1,0:T(8,128)(2,1)S(1)} %bitcast.197, bf16[768,16]{0,1:T(8,128)(2,1)S(1)} %copy-done.12, bf16[768,16]{0,1:T(8,128)(2,1)S(1)} %copy-done.14), kind=kOutput, calls=%fused_computation.9 | convolution fusion | flops 214532096 | bytes 31768576 | tf_op jit(solution)/shard_map/dot_general | solution.py:19
  625.9 10.6 %pad_maximum_fusion = bf16[16,96,4224]{2,1,0:T(8,128)(2,1)} fusion(bf16[16,96,128]{2,1,0:T(8,128)(2,1)S(1)} %fusion.46, bf16[16,48,4096]{2,1,0:T(8,128)(2,1)} %bitcast.178, bf16[16,48,4096]{2,1,0:T(8,128)(2,1)S(1)} %bitcast.174), kind=kLoop, calls=%fused_computation.6 | loop fusion | flops 38928384 | bytes 25952256 | tf_op jit(solution)/shard_map/concatenate | solution.py:230
  643.2 5.6 fusion.93
  648.7 5.6 fusion.92
  654.3 8.7 %pad_maximum_fusion.2 = bf16[16,96,4096]{2,1,0:T(8,128)(2,1)} fusion(bf16[16,48,4096]{2,1,0:T(8,128)(2,1)S(1)} %bitcast.176, bf16[16,48,4096]{2,1,0:T(8,128)(2,1)S(1)} %bitcast.179), kind=kLoop, calls=%fused_computation.8 | loop fusion | flops 25165824 | bytes 25165824 | tf_op jit(solution)/shard_map/concatenate | solution.py:237
  663.1 8.6 %pad_maximum_fusion.1 = bf16[16,96,4096]{2,1,0:T(8,128)(2,1)} fusion(bf16[16,48,4096]{2,1,0:T(8,128)(2,1)S(1)} %bitcast.175, bf16[16,48,4096]{2,1,0:T(8,128)(2,1)S(1)} %bitcast.177), kind=kLoop, calls=%fused_computation.7 | loop fusion | flops 25165824 | bytes 25165824 | tf_op jit(solution)/shard_map/concatenate | solution.py:236
  671.6 72.0 %reduce-scatter.4.cloned.1.call-done = bf16[1,96,4224]{2,1,0:T(8,128)(2,1)} async-done(((bf16[16,96,4224]{2,1,0:T(8,128)(2,1)}), bf16[1,96,4224]{2,1,0:T(8,128)(2,1)}) %reduce-scatter.4.cloned.1.call-update) | async-done | bytes 811024
  745.6 16.5 %all-gather = bf16[16,96,48]{1,2,0:T(8,128)(2,1)S(1)} all-gather(bf16[1,96,48]{1,2,0:T(8,128)(2,1)S(1)} %copy.88), channel_id=1, replica_groups=mesh['dp'=16,'expert'=8] {'dp'}, dimensions={0}, use_global_device_ids=true | all-gather | bytes 156672 | tf_op jit(solution)/shard_map/all_gather | solution.py:234
  762.4 7.2 fusion.1
  774.2 11.4 %all-to-all-start.3 = ((bf16[96,8,512]{2,0,1:T(8,128)(2,1)}), bf16[96,8,512]{2,0,1:T(8,128)(2,1)S(1)}, u32[]{:S(2)}, u32[]{:S(2)}) async-start(bf16[96,8,512]{2,0,1:T(8,128)(2,1)} %bitcast.168), calls=%async_computation.3 | async-start | bytes 1572864 | tf_op jit(solution)/shard_map/all_to_all | solution.py:244
  785.5 7.1 fusion
  792.6 5.2 all-to-all-done.3
  (137 shorter events, 66.7 us)
Async XLA Ops:
  7.2 519.2 %copy-start = (bf16[1,4096,16]{1,2,0:T(8,128)(2,1)S(1)}, bf16[1,4096,16]{1,2,0:T(8,128)(2,1)}, u32[]{:S(2)}) copy-start(bf16[1,4096,16]{1,2,0:T(8,128)(2,1)} %param.25) | copy-start | bytes 393220
  65.1 226.3 %all-to-all-start.2 = ((bf16[16,48,8192]{2,1,0:T(8,128)(2,1)}), bf16[16,48,8192]{2,1,0:T(8,128)(2,1)}, u32[]{:S(2)}, u32[]{:S(2)}) async-start(bf16[16,48,8192]{2,1,0:T(8,128)(2,1)} %stack.11), calls=%async_computation.2 | async-start | bytes 25165824 | tf_op jit(solution)/shard_map/all_to_all | solution.py:14
  297.5 12.7 %copy-start.6 = (bf16[1,16,4096]{2,1,0:T(8,128)(2,1)S(1)}, bf16[1,16,4096]{2,1,0:T(8,128)(2,1)}, u32[]{:S(2)}) copy-start(bf16[1,16,4096]{2,1,0:T(8,128)(2,1)} %param.22) | copy-start | bytes 393220
  297.5 219.8 %all-to-all-start.1 = ((bf16[16,48,8192]{2,1,0:T(8,128)(2,1)}), bf16[16,48,8192]{2,1,0:T(8,128)(2,1)}, u32[]{:S(2)}, u32[]{:S(2)}) async-start(bf16[16,48,8192]{2,1,0:T(8,128)(2,1)} %stack.9), calls=%async_computation.1 | async-start | bytes 25165824 | tf_op jit(solution)/shard_map/all_to_all | solution.py:14
  309.9 4.8 copy-start.7
  309.9 433.7 %reduce-scatter.4.cloned.1.call-start = ((), (), s32[]{:S(2)}) async-start(), calls=%async_computation.5 | async-start | bytes 13787136
  314.7 273.2 %copy-start.15 = (bf16[768,16]{0,1:T(8,128)(2,1)}, bf16[768,16]{0,1:T(8,128)(2,1)S(1)}, u32[]{:S(2)}) copy-start(bf16[768,16]{0,1:T(8,128)(2,1)S(1)} %convolution_convert_fusion.7) | copy-start | bytes 73732
  319.3 269.1 %copy-start.24 = (bf16[768,16]{0,1:T(8,128)(2,1)}, bf16[768,16]{0,1:T(8,128)(2,1)S(1)}, u32[]{:S(2)}) copy-start(bf16[768,16]{0,1:T(8,128)(2,1)S(1)} %convolution_convert_fusion.6) | copy-start | bytes 73732
  521.8 50.1 %copy-start.17 = (bf16[768,16]{0,1:T(8,128)(2,1)}, bf16[768,16]{0,1:T(8,128)(2,1)S(1)}, u32[]{:S(2)}) copy-start(bf16[768,16]{0,1:T(8,128)(2,1)S(1)} %convolution_convert_fusion.10) | copy-start | bytes 73732
  526.3 46.1 %copy-start.26 = (bf16[768,16]{0,1:T(8,128)(2,1)}, bf16[768,16]{0,1:T(8,128)(2,1)S(1)}, u32[]{:S(2)}) copy-start(bf16[768,16]{0,1:T(8,128)(2,1)S(1)} %convolution_convert_fusion.9) | copy-start | bytes 73732
  530.9 56.7 %copy-start.19 = (bf16[768,16]{0,1:T(8,128)(2,1)}, bf16[768,16]{0,1:T(8,128)(2,1)S(1)}, u32[]{:S(2)}) copy-start(bf16[768,16]{0,1:T(8,128)(2,1)S(1)} %convolution_convert_fusion.8) | copy-start | bytes 73732
  530.9 4.7 copy-start.4
  535.5 35.9 %copy-start.21 = (bf16[768,16]{0,1:T(8,128)(2,1)}, bf16[768,16]{0,1:T(8,128)(2,1)S(1)}, u32[]{:S(2)}) copy-start(bf16[768,16]{0,1:T(8,128)(2,1)S(1)} %convolution_convert_fusion.11) | copy-start | bytes 73732
  541.4 6.5 copy-start.28
  553.7 6.0 copy-start.3
  565.5 5.9 copy-start.9
  565.5 6.3 copy-start.8
  565.6 6.9 copy-start.23
  581.1 23.1 %copy-start.10 = (bf16[768,16]{0,1:T(8,128)(2,1)}, bf16[768,16]{0,1:T(8,128)(2,1)S(1)}, u32[]{:S(2)}) copy-start(bf16[768,16]{0,1:T(8,128)(2,1)S(1)} %convolution_convert_fusion.5) | copy-start | bytes 73732
  589.4 13.2 %copy-start.5 = (bf16[448,768]{1,0:T(8,128)(2,1)}, bf16[448,768]{1,0:T(8,128)(2,1)S(1)}, u32[]{:S(2)}) copy-start(bf16[448,768]{1,0:T(8,128)(2,1)S(1)} %get-tuple-element.15) | copy-start | bytes 2064388
  589.6 13.2 %copy-start.11 = (bf16[768,16]{0,1:T(8,128)(2,1)}, bf16[768,16]{0,1:T(8,128)(2,1)S(1)}, u32[]{:S(2)}) copy-start(bf16[768,16]{0,1:T(8,128)(2,1)S(1)} %convolution_convert_fusion.2) | copy-start | bytes 73732
  596.2 6.6 copy-start.13
  604.6 9.3 %copy-start.12 = (bf16[768,16]{0,1:T(8,128)(2,1)S(1)}, bf16[768,16]{0,1:T(8,128)(2,1)}, u32[]{:S(2)}) copy-start(bf16[768,16]{0,1:T(8,128)(2,1)} %copy-done.11) | copy-start | bytes 73732
  604.6 9.3 %copy-start.14 = (bf16[768,16]{0,1:T(8,128)(2,1)S(1)}, bf16[768,16]{0,1:T(8,128)(2,1)}, u32[]{:S(2)}) copy-start(bf16[768,16]{0,1:T(8,128)(2,1)} %copy-done.13) | copy-start | bytes 73732
  636.5 2.1 copy-start.20
  636.5 4.2 copy-start.27
  636.5 4.4 copy-start.25
  636.5 5.4 copy-start.18
  636.5 5.7 copy-start.16
  762.4 8.3 %copy-start.2 = (bf16[16,96,4096]{2,1,0:T(8,128)(2,1)S(1)}, bf16[16,96,4096]{2,1,0:T(8,128)(2,1)}, u32[]{:S(2)}) copy-start(bf16[16,96,4096]{2,1,0:T(8,128)(2,1)} %pad_maximum_fusion.1) | copy-start | bytes 37748740
  774.2 23.7 %all-to-all-start.3 = ((bf16[96,8,512]{2,0,1:T(8,128)(2,1)}), bf16[96,8,512]{2,0,1:T(8,128)(2,1)S(1)}, u32[]{:S(2)}, u32[]{:S(2)}) async-start(bf16[96,8,512]{2,0,1:T(8,128)(2,1)} %bitcast.168), calls=%async_computation.3 | async-start | bytes 1572864 | tf_op jit(solution)/shard_map/all_to_all | solution.py:244
  785.5 15.4 %copy-start.1 = (bf16[1,4096,16]{1,2,0:T(8,128)(2,1)S(1)}, bf16[1,4096,16]{1,2,0:T(8,128)(2,1)}, u32[]{:S(2)}) copy-start(bf16[1,4096,16]{1,2,0:T(8,128)(2,1)} %param.25) | copy-start | bytes 393220
  (1 other events, 0.7 us)
Sparse Core Ops, SparseCore 0:
  636.7 106.9 reduce-scatter.3
